TPU v7x, 32 devices: a whole 2x2x4 slice. The times are simulated.
32 devices in a mesh: dp: 8 (over z, y), tensor: 4 (over x, core).
Axes of the slice: x: 2, y: 2, z: 4, core: 2. Of those that a mesh axis runs over, the one named last changes fastest.
Arguments:
- tokens: bfloat16 [4096, 2048], P(('dp', 'tensor')), may hold values from -6 to 6
- lengths: int32 [8, 4], P('dp'), may hold values from 0 to 512, as said below
- w_query: bfloat16 [2048, 2048], P(None, 'tensor'), may hold values from -0.125 to 0.125
- w_key: bfloat16 [2048, 2048], P(None, 'tensor'), may hold values from -0.125 to 0.125
- w_value: bfloat16 [2048, 2048], P(None, 'tensor'), may hold values from -0.125 to 0.125
- w_out: bfloat16 [2048, 2048], P('tensor'), may hold values from -0.125 to 0.125
- w_gate: bfloat16 [2048, 8192], P(None, 'tensor'), may hold values from -0.125 to 0.125
- w_up: bfloat16 [2048, 8192], P(None, 'tensor'), may hold values from -0.125 to 0.125
- w_down: bfloat16 [8192, 2048], P('tensor'), may hold values from -0.0625 to 0.0625
- gain_query: float32 [2048], P('tensor'), may hold values from 0.1 to 1.9
- gain_key: float32 [2048], P('tensor'), may hold values from 0.1 to 1.9
- gain_attn: float32 [2048], replicated, may hold values from 0.1 to 1.9
- gain_mlp: float32 [2048], replicated, may hold values from 0.1 to 1.9
- cotangent: bfloat16 [4096, 2048], P(('dp', 'tensor')), may hold values from -6 to 6
Outputs:
- output: bfloat16 [4096, 2048], P(('dp', 'tensor'))
- grad_tokens: bfloat16 [4096, 2048], P(('dp', 'tensor'))
- grad_w_query: float32 [2048, 2048], P('dp', 'tensor')
- grad_w_key: float32 [2048, 2048], P('dp', 'tensor')
- grad_w_value: float32 [2048, 2048], P('dp', 'tensor')
- grad_w_out: float32 [2048, 2048], P('tensor', 'dp')
- grad_w_gate: float32 [2048, 8192], P('dp', 'tensor')
- grad_w_up: float32 [2048, 8192], P('dp', 'tensor')
- grad_w_down: float32 [8192, 2048], P('tensor', 'dp')
- grad_gain_query: float32 [2048], P('tensor')
- grad_gain_key: float32 [2048], P('tensor')
- grad_gain_attn: float32 [2048], replicated
- grad_gain_mlp: float32 [2048], replicated
Inputs may be any that keep to these rules, and one draw needn't show every extreme that they name: Each row lists the lengths of its sequences in order, then zeros; every nonzero length is 128 or more and they sum to 512; row 0 holds one sequence of 512 tokens.
All inputs are finite; a program needn't handle non-finite values.
Results may differ from a plain program's by a relative error of at most 0.023.
Values may be sent and summed in bfloat16 or wider, within the bound.
A program may use at most 256 MiB of HBM per device.

v0:
```python
import math
import jax
import jax.numpy as jnp
from jax import lax
from jax.sharding import PartitionSpec as P

HD = 128
ROW_LEN = 512
EPS = 1e-06
THETA = 500000.0


def rotate(values, offsets, rot_sign):
    half_width = values.shape[-1] // 2
    frequency = jnp.exp(
        jnp.arange(half_width, dtype=jnp.float32) * (-2.0 * math.log(THETA) / values.shape[-1])
    )
    angles = offsets.astype(jnp.float32)[..., None, None] * frequency
    cosines = jnp.cos(angles)
    sine_part = rot_sign * jnp.sin(angles)
    first_half = values[..., :half_width]
    second_half = values[..., half_width:]
    return jnp.concatenate(
        [
            first_half * cosines - second_half * sine_part,
            second_half * cosines + first_half * sine_part,
        ],
        axis=-1,
    )


def row_layout(lengths_row):
    slots = jnp.arange(lengths_row.shape[0], dtype=jnp.int32)
    seq_ends = jnp.sum(jnp.where(slots[None, :] <= slots[:, None], lengths_row[None, :], 0), axis=1)
    position = jnp.arange(ROW_LEN, dtype=jnp.int32)
    passed = (position[:, None] >= seq_ends[None, :]).astype(jnp.int32)
    segment = jnp.sum(passed, axis=1)
    seq_start = jnp.sum(passed * lengths_row[None, :], axis=1)
    return (segment, position - seq_start)


def allowed_mask(segment):
    position = jnp.arange(segment.shape[0], dtype=jnp.int32)
    return (segment[:, None] == segment[None, :]) & (position[None, :] <= position[:, None])


def times_t(left_mat, right_mat):
    return lax.dot_general(
        left_mat, right_mat, (((1,), (1,)), ((), ())), preferred_element_type=jnp.float32
    )


def t_times(left_mat, right_mat):
    return lax.dot_general(
        left_mat, right_mat, (((0,), (0,)), ((), ())), preferred_element_type=jnp.float32
    )


def masked_scores(queries_low, keys_low, segment):
    scale_factor = 1.0 / math.sqrt(queries_low.shape[-1])
    scores = (
        jnp.einsum("qhd,khd->hqk", queries_low, keys_low, preferred_element_type=jnp.float32)
        * scale_factor
    )
    return jnp.where(allowed_mask(segment)[None], scores, -1e30)


def attend(block_item):
    queries_low, keys_low, values_low, segment = block_item
    scores = masked_scores(queries_low, keys_low, segment)
    row_max = jnp.max(scores, axis=-1, keepdims=True)
    shifted = jnp.exp(scores - row_max)
    row_total = jnp.sum(shifted, axis=-1, keepdims=True)
    attn_weights = (shifted / row_total).astype(jnp.bfloat16)
    mixed = jnp.einsum("hqk,khd->qhd", attn_weights, values_low, preferred_element_type=jnp.float32)
    return (mixed.astype(jnp.bfloat16), (row_max + jnp.log(row_total))[..., 0])


def attend_back(block_item):
    queries_low, keys_low, values_low, segment, log_total, grad_mixed = block_item
    scale_factor = 1.0 / math.sqrt(queries_low.shape[-1])
    scores = masked_scores(queries_low, keys_low, segment)
    attn_weights = jnp.exp(scores - log_total[..., None])
    grad_weights = jnp.einsum(
        "qhd,khd->hqk", grad_mixed, values_low, preferred_element_type=jnp.float32
    )
    row_dots = jnp.sum(attn_weights * grad_weights, axis=-1, keepdims=True)
    grad_scores = (attn_weights * (grad_weights - row_dots)).astype(jnp.bfloat16)
    grad_queries = scale_factor * jnp.einsum(
        "hqk,khd->qhd", grad_scores, keys_low, preferred_element_type=jnp.float32
    )
    grad_keys = scale_factor * jnp.einsum(
        "hqk,qhd->khd", grad_scores, queries_low, preferred_element_type=jnp.float32
    )
    grad_values = jnp.einsum(
        "hqk,qhd->khd",
        attn_weights.astype(jnp.bfloat16),
        grad_mixed,
        preferred_element_type=jnp.float32,
    )
    return (grad_queries, grad_keys, grad_values.astype(jnp.bfloat16))


def post_norm_back(grad_in, unit_rows, inv_scale, gain_vec):
    scaled = grad_in * gain_vec
    mean_dots = jnp.mean(scaled * unit_rows, axis=-1, keepdims=True)
    return (inv_scale * (scaled - unit_rows * mean_dots), jnp.sum(grad_in * unit_rows, axis=0))


OUTER = 4


def swap(value, shift):
    size = lax.axis_size("dp")
    return lax.ppermute(value, "dp", [(d, d ^ shift) for d in range(size)])


def pick(parts, index):
    return lax.dynamic_index_in_dim(parts, index, 0, keepdims=False)


def sum_inner(parts):
    inner = parts.shape[0]
    mine = lax.axis_index("dp") % inner
    total = pick(parts, mine)
    for k in range(1, inner):
        sent = pick(parts, mine ^ k).astype(jnp.bfloat16)
        total = total + swap(sent, k).astype(jnp.float32)
    return total


def trade_outer(parts, inner):
    mine = lax.axis_index("dp") // inner
    got = [(mine, pick(parts, mine))]
    for k in range(1, OUTER):
        got.append((mine ^ k, swap(pick(parts, mine ^ k), k * inner)))
    return got


def split_rows(grad, inner):
    cols = grad.shape[1]
    return grad.reshape(OUTER, inner, -1, cols).transpose(1, 0, 2, 3)


def split_cols(grad, inner):
    rows = grad.shape[0]
    return grad.reshape(rows, OUTER, inner, -1).transpose(2, 1, 0, 3)


def scatter_sum(parts, inner):
    half = sum_inner(parts).astype(jnp.bfloat16)
    got = trade_outer(half, inner)
    return sum((g.astype(jnp.float32) for _, g in got))


def scatter_join(parts, inner, axis):
    half = sum_inner(parts).astype(jnp.bfloat16)
    got = trade_outer(half, inner)
    stack = jnp.zeros((OUTER, *got[0][1].shape), jnp.bfloat16)
    for place, block in got:
        stack = lax.dynamic_update_index_in_dim(stack, block, place, 0)
    joined = jnp.concatenate([stack[z] for z in range(OUTER)], axis=axis)
    return joined.astype(jnp.float32)


def body(
    tokens,
    lengths,
    w_query,
    w_key,
    w_value,
    w_out,
    w_gate,
    w_up,
    w_down,
    gain_query,
    gain_key,
    gain_attn,
    gain_mlp,
    cotangent,
):
    rows_dev = lengths.shape[0]
    model_width = w_query.shape[0]
    local_width = w_query.shape[1]
    head_count = local_width // HD
    gathered = lax.all_gather(tokens, "tensor", axis=0, tiled=True)
    row_count = gathered.shape[0]
    segment, offsets = jax.vmap(row_layout)(lengths)
    queries = jnp.dot(gathered, w_query, preferred_element_type=jnp.float32)
    keys_raw = jnp.dot(gathered, w_key, preferred_element_type=jnp.float32)
    values_low = jnp.dot(gathered, w_value, preferred_element_type=jnp.float32).astype(jnp.bfloat16)
    q_total, k_total = lax.psum(
        (jnp.sum(queries * queries, axis=1), jnp.sum(keys_raw * keys_raw, axis=1)), "tensor"
    )
    q_inv = lax.rsqrt(q_total / model_width + EPS)[:, None]
    k_inv = lax.rsqrt(k_total / model_width + EPS)[:, None]
    q_unit = queries * q_inv
    k_unit = keys_raw * k_inv

    def to_heads(values):
        return values.reshape(rows_dev, ROW_LEN, head_count, HD)

    queries_low = rotate(to_heads(q_unit * gain_query), offsets, 1.0).astype(jnp.bfloat16)
    keys_low = rotate(to_heads(k_unit * gain_key), offsets, 1.0).astype(jnp.bfloat16)
    values_heads = to_heads(values_low)
    mixed_heads, log_total = jax.vmap(lambda *a: attend(a))(
        queries_low, keys_low, values_heads, segment
    )
    mixed_low = mixed_heads.reshape(row_count, local_width)
    attn_out = lax.psum_scatter(
        jnp.dot(mixed_low, w_out, preferred_element_type=jnp.float32).astype(jnp.bfloat16),
        "tensor",
        scatter_dimension=0,
        tiled=True,
    ).astype(jnp.float32)
    a_inv = lax.rsqrt(jnp.mean(attn_out * attn_out, axis=1, keepdims=True) + EPS)
    a_unit = attn_out * a_inv
    hidden = tokens.astype(jnp.float32) + a_unit * gain_attn
    hidden_low = hidden.astype(jnp.bfloat16)
    hidden_all = lax.all_gather(hidden_low, "tensor", axis=0, tiled=True)
    inner_count = lax.axis_size("dp") // OUTER
    outer_index = lax.axis_index("dp") // inner_count

    def gather_group(shard):
        groups = [[z * inner_count + i for z in range(OUTER)] for i in range(inner_count)]
        part = lax.all_gather(shard, "dp", axis=0, tiled=True, axis_index_groups=groups)
        return lax.all_gather(part, "tensor", axis=0, tiled=True)

    hidden_group = gather_group(hidden_low)
    gate_acts = jnp.dot(hidden_all, w_gate, preferred_element_type=jnp.float32)
    up_acts = jnp.dot(hidden_all, w_up, preferred_element_type=jnp.float32)
    gate_sigmoid = jax.nn.sigmoid(gate_acts)
    inner_low = (gate_acts * gate_sigmoid * up_acts).astype(jnp.bfloat16)
    mlp_out = lax.psum_scatter(
        jnp.dot(inner_low, w_down, preferred_element_type=jnp.float32).astype(jnp.bfloat16),
        "tensor",
        scatter_dimension=0,
        tiled=True,
    ).astype(jnp.float32)
    f_inv = lax.rsqrt(jnp.mean(mlp_out * mlp_out, axis=1, keepdims=True) + EPS)
    f_unit = mlp_out * f_inv
    output = (hidden + f_unit * gain_mlp).astype(jnp.bfloat16)
    grad_output = cotangent.astype(jnp.float32)
    grad_mlp, grad_gain_mlp_part = post_norm_back(grad_output, f_unit, f_inv, gain_mlp)
    grad_mlp_low = grad_mlp.astype(jnp.bfloat16)
    mlp_grad_all = lax.all_gather(grad_mlp_low, "tensor", axis=0, tiled=True)
    mlp_grad_group = gather_group(grad_mlp_low)
    grad_inner = times_t(mlp_grad_all, w_down)
    grad_gate_low = (
        grad_inner * up_acts * gate_sigmoid * (1.0 + gate_acts * (1.0 - gate_sigmoid))
    ).astype(jnp.bfloat16)
    grad_up_low = (grad_inner * gate_acts * gate_sigmoid).astype(jnp.bfloat16)
    part_width = w_gate.shape[1] // OUTER
    gate_part = lax.dynamic_slice_in_dim(w_gate, outer_index * part_width, part_width, 1)
    up_part = lax.dynamic_slice_in_dim(w_up, outer_index * part_width, part_width, 1)
    down_part = lax.dynamic_slice_in_dim(w_down, outer_index * part_width, part_width, 0)
    gate_g = jnp.dot(hidden_group, gate_part, preferred_element_type=jnp.float32)
    up_g = jnp.dot(hidden_group, up_part, preferred_element_type=jnp.float32)
    sig_g = jax.nn.sigmoid(gate_g)
    inner_g = (gate_g * sig_g * up_g).astype(jnp.bfloat16)
    grad_inner_g = times_t(mlp_grad_group, down_part)
    grad_gate_g = (grad_inner_g * up_g * sig_g * (1.0 + gate_g * (1.0 - sig_g))).astype(
        jnp.bfloat16
    )
    grad_up_g = (grad_inner_g * gate_g * sig_g).astype(jnp.bfloat16)
    sum_down = scatter_join(
        split_cols(t_times(inner_g, mlp_grad_group), inner_count), inner_count, 0
    )
    sum_gate = scatter_join(
        split_rows(t_times(hidden_group, grad_gate_g), inner_count), inner_count, 1
    )
    sum_up = scatter_join(split_rows(t_times(hidden_group, grad_up_g), inner_count), inner_count, 1)
    grad_hidden = grad_output + lax.psum_scatter(
        (times_t(grad_gate_low, w_gate) + times_t(grad_up_low, w_up)).astype(jnp.bfloat16),
        "tensor",
        scatter_dimension=0,
        tiled=True,
    ).astype(jnp.float32)
    grad_attn, grad_gain_attn_part = post_norm_back(grad_hidden, a_unit, a_inv, gain_attn)
    attn_grad_all = lax.all_gather(grad_attn.astype(jnp.bfloat16), "tensor", axis=0, tiled=True)
    grad_w_out = t_times(mixed_low, attn_grad_all)
    grad_mixed = times_t(attn_grad_all, w_out).astype(jnp.bfloat16)
    grad_q_rot, grad_k_rot, grad_values_low = jax.vmap(lambda *a: attend_back(a))(
        queries_low, keys_low, values_heads, segment, log_total, to_heads(grad_mixed)
    )
    grad_q_norm = rotate(grad_q_rot, offsets, -1.0).reshape(row_count, local_width)
    grad_k_norm = rotate(grad_k_rot, offsets, -1.0).reshape(row_count, local_width)
    grad_gain_query_part = jnp.sum(grad_q_norm * q_unit, axis=0)
    grad_gain_key_part = jnp.sum(grad_k_norm * k_unit, axis=0)
    q_scaled = grad_q_norm * gain_query
    k_scaled = grad_k_norm * gain_key
    q_dots, k_dots = lax.psum(
        (jnp.sum(q_scaled * q_unit, axis=1), jnp.sum(k_scaled * k_unit, axis=1)), "tensor"
    )
    grad_queries_low = (q_inv * (q_scaled - q_unit * (q_dots / model_width)[:, None])).astype(
        jnp.bfloat16
    )
    grad_keys_low = (k_inv * (k_scaled - k_unit * (k_dots / model_width)[:, None])).astype(
        jnp.bfloat16
    )
    grad_values_flat = grad_values_low.reshape(row_count, local_width)
    grad_w_query = t_times(gathered, grad_queries_low)
    grad_w_key = t_times(gathered, grad_keys_low)
    grad_w_value = t_times(gathered, grad_values_flat)
    grad_tokens = (
        grad_hidden
        + lax.psum_scatter(
            (
                times_t(grad_queries_low, w_query)
                + times_t(grad_keys_low, w_key)
                + times_t(grad_values_flat, w_value)
            ).astype(jnp.bfloat16),
            "tensor",
            scatter_dimension=0,
            tiled=True,
        ).astype(jnp.float32)
    ).astype(jnp.bfloat16)
    tensor_start = lax.axis_index("tensor") * local_width
    zero_row = jnp.zeros((model_width,), jnp.float32)
    q_full = lax.dynamic_update_slice(zero_row, grad_gain_query_part, (tensor_start,))
    k_full = lax.dynamic_update_slice(zero_row, grad_gain_key_part, (tensor_start,))
    gain_stack = jnp.stack([q_full, k_full, grad_gain_attn_part, grad_gain_mlp_part])
    gain_total = lax.psum(gain_stack, ("dp", "tensor"))
    grad_gain_query = lax.dynamic_slice(gain_total[0], (tensor_start,), (local_width,))
    grad_gain_key = lax.dynamic_slice(gain_total[1], (tensor_start,), (local_width,))
    summed = (
        scatter_sum(split_rows(grad_w_query, inner_count), inner_count),
        scatter_sum(split_rows(grad_w_key, inner_count), inner_count),
        scatter_sum(split_rows(grad_w_value, inner_count), inner_count),
        scatter_sum(split_cols(grad_w_out, inner_count), inner_count),
        sum_gate,
        sum_up,
        sum_down,
    )
    return (
        output,
        grad_tokens,
        summed[0],
        summed[1],
        summed[2],
        summed[3],
        summed[4],
        summed[5],
        summed[6],
        grad_gain_query,
        grad_gain_key,
        gain_total[2],
        gain_total[3],
    )


def solution(mesh):
    placed = (
        P(("dp", "tensor"), None),
        P("dp", None),
        P(None, "tensor"),
        P(None, "tensor"),
        P(None, "tensor"),
        P("tensor", None),
        P(None, "tensor"),
        P(None, "tensor"),
        P("tensor", None),
        P("tensor"),
        P("tensor"),
        P(),
        P(),
        P(("dp", "tensor"), None),
    )
    return jax.shard_map(
        body,
        mesh=mesh,
        in_specs=placed,
        out_specs=(
            P(("dp", "tensor"), None),
            P(("dp", "tensor"), None),
            P("dp", "tensor"),
            P("dp", "tensor"),
            P("dp", "tensor"),
            P("tensor", "dp"),
            P("dp", "tensor"),
            P("dp", "tensor"),
            P("tensor", "dp"),
            P("tensor"),
            P("tensor"),
            P(),
            P(),
        ),
        check_vma=False,
    )
```

profile of v0, /device:TPU:9, one launch (start us, length us, event | category | flops | bytes accessed | tf_op | source)
XLA Modules:
  0.0 888.0 jit_solution(406805340475882868)
XLA Ops:
  12.2 21.6 %all-gather.9.cloned.1.call-done = bf16[512,2048]{1,0:T(8,128)(2,1)} async-done(((bf16[128,2048]{1,0:T(8,128)(2,1)}), bf16[512,2048]{1,0:T(8,128)(2,1)}) %all-gather.9.cloned.1.call-update) | async-done | bytes 2097168 | tf_op jit(solution)/shard_map/all_gather | solution.py:186
  70.3 32.8 %reduce-scatter.5.cloned.1.call-done = bf16[128,2048]{1,0:T(8,128)(2,1)} async-done(((bf16[512,2048]{1,0:T(8,128)(2,1)}), bf16[128,2048]{1,0:T(8,128)(2,1)}) %reduce-scatter.5.cloned.1.call-update) | async-done | bytes 524304 | tf_op jit(solution)/shard_map/reduce_scatter | solution.py:210
  106.8 22.8 %all-gather.11.cloned.1.call-done = bf16[512,2048]{1,0:T(8,128)(2,1)} async-done(((bf16[128,2048]{1,0:T(8,128)(2,1)}), bf16[512,2048]{1,0:T(8,128)(2,1)}) %all-gather.11.cloned.1.call-update) | async-done | bytes 2097168 | tf_op jit(solution)/shard_map/all_gather | solution.py:220
  129.6 8.6 fusion.92
  138.2 8.4 fusion.93
  148.6 9.5 %convolution_convert_fusion = bf16[512,2048]{1,0:T(8,128)(2,1)} fusion(bf16[2048,2048]{1,0:T(8,128)(2,1)} %param.22, f32[512,2048]{1,0:T(8,128)S(1)} %fusion.93, f32[512,2048]{1,0:T(8,128)S(1)} %fusion.92), kind=kOutput, calls=%fused_computation.21 | convolution fusion | flops 4302307328 | bytes 18874368 | tf_op jit(solution)/shard_map/dot_general | solution.py:235
  158.2 31.1 %reduce-scatter.7.cloned.1.call-done = bf16[128,2048]{1,0:T(8,128)(2,1)} async-done(((bf16[512,2048]{1,0:T(8,128)(2,1)}), bf16[128,2048]{1,0:T(8,128)(2,1)}) %reduce-scatter.7.cloned.1.call-update) | async-done | bytes 524304 | tf_op jit(solution)/shard_map/reduce_scatter | solution.py:234
  194.3 23.1 %all-gather.13.cloned.1.call-done = bf16[512,2048]{1,0:T(8,128)(2,1)} async-done(((bf16[128,2048]{1,0:T(8,128)(2,1)}), bf16[512,2048]{1,0:T(8,128)(2,1)}) %all-gather.13.cloned.1.call-update) | async-done | bytes 2097168 | tf_op jit(solution)/shard_map/all_gather | solution.py:246
  217.4 7.6 fusion.94
  225.0 13.6 %fusion.25 = f32[512,2048]{1,0:T(8,128)} fusion(bf16[2048,2048]{1,0:T(8,128)(2,1)} %param.20, f32[512,2048]{1,0:T(8,128)} %copy-done.53, f32[512,2048]{1,0:T(8,128)S(1)} %fusion.94, f32[512,2048]{1,0:T(8,128)} %copy-done.54), kind=kOutput, calls=%fused_computation.56 | convolution fusion | flops 4305453056 | bytes 25165824 | tf_op jit(solution)/shard_map/dot_general | solution.py:48
  238.6 11.8 %add_convert_fusion.1 = bf16[512,2048]{1,0:T(8,128)(2,1)} fusion(f32[512,2048]{1,0:T(8,128)} %fusion.25, bf16[2048,2048]{1,0:T(8,128)(2,1)} %param.21, f32[512,2048]{1,0:T(8,128)S(1)} %fusion.94, f32[512,2048]{1,0:T(8,128)} %copy-done.53), kind=kOutput, calls=%fused_computation.8 | convolution fusion | flops 4303355904 | bytes 23068672 | tf_op jit(solution)/shard_map/dot_general | solution.py:48
  251.3 30.4 %reduce-scatter.9.cloned.1.call-done = bf16[128,2048]{1,0:T(8,128)(2,1)} async-done(((bf16[512,2048]{1,0:T(8,128)(2,1)}), bf16[128,2048]{1,0:T(8,128)(2,1)}) %reduce-scatter.9.cloned.1.call-update) | async-done | bytes 524304 | tf_op jit(solution)/shard_map/reduce_scatter | solution.py:273
  286.9 41.1 %all-gather.17.cloned.1.call-done = bf16[512,2048]{1,0:T(8,128)(2,1)} async-done(((bf16[128,2048]{1,0:T(8,128)(2,1)}), bf16[512,2048]{1,0:T(8,128)(2,1)}) %all-gather.17.cloned.1.call-update) | async-done | bytes 2097168 | tf_op jit(solution)/shard_map/all_gather | solution.py:226
  328.2 25.5 %all-gather.15.cloned.1.call-done = bf16[512,2048]{1,0:T(8,128)(2,1)} async-done(((bf16[128,2048]{1,0:T(8,128)(2,1)}), bf16[512,2048]{1,0:T(8,128)(2,1)}) %all-gather.15.cloned.1.call-update) | async-done | bytes 2097168 | tf_op jit(solution)/shard_map/all_gather | solution.py:280
  399.8 60.7 %all-gather.19.cloned.1.call-done = bf16[2048,2048]{1,0:T(8,128)(2,1)} async-done(((bf16[512,2048]{1,0:T(8,128)(2,1)}), bf16[2048,2048]{1,0:T(8,128)(2,1)}) %all-gather.19.cloned.1.call-update) | async-done | bytes 8388624 | tf_op jit(solution)/shard_map/all_gather | solution.py:227
  460.5 10.6 %fusion.14 = f32[2048,512]{1,0:T(8,128)} fusion(bf16[2048,2048]{1,0:T(8,128)(2,1)} %all-gather.19.cloned.1.call-done, bf16[2048,2048]{1,0:T(8,128)(2,1)} %param.20, s32[]{:T(128)S(6)} %select_n.141), kind=kOutput, calls=%fused_computation.44 | convolution fusion | flops 4294967296 | bytes 14680068 | tf_op jit(solution)/shard_map/dot_general | solution.py:257
  471.2 8.7 fusion.18
  505.5 6.8 reshape.573
  527.1 6.8 reshape.574
  554.8 71.2 %psum.39 = f32[4,2048]{1,0:T(4,128)S(1)} all-reduce(f32[4,2048]{1,0:T(4,128)S(1)} %pad_maximum_fusion.8), channel_id=1, replica_groups=mesh['dp'=8,'tensor'=4] {'dp','tensor'}, use_global_device_ids=true, to_apply=%region_26.27 | all-reduce | flops 8192 | bytes 65536 | tf_op jit(solution)/shard_map/psum | solution.py:323
  668.2 14.5 %collective-permute-done.2 = bf16[256,512]{1,0:T(8,128)(2,1)S(1)} collective-permute-done((bf16[256,512]{1,0:T(8,128)(2,1)S(1)}, bf16[256,512]{1,0:T(8,128)(2,1)S(1)}, u32[]{:S(2)}, u32[]{:S(2)}) %collective-permute-start.2) | collective-permute-done | bytes 262176 | tf_op jit(solution)/shard_map/ppermute | solution.py:115
  688.4 13.6 %collective-permute-done.7 = bf16[256,512]{1,0:T(8,128)(2,1)S(1)} collective-permute-done((bf16[256,512]{1,0:T(8,128)(2,1)S(1)}, bf16[256,512]{1,0:T(8,128)(2,1)S(1)}, u32[]{:S(2)}, u32[]{:S(2)}) %collective-permute-start.7) | collective-permute-done | bytes 262176 | tf_op jit(solution)/shard_map/ppermute | solution.py:115
  710.9 13.6 %collective-permute-done.11 = bf16[256,512]{1,0:T(8,128)(2,1)S(1)} collective-permute-done((bf16[256,512]{1,0:T(8,128)(2,1)S(1)}, bf16[256,512]{1,0:T(8,128)(2,1)S(1)}, u32[]{:S(2)}, u32[]{:S(2)}) %collective-permute-start.11) | collective-permute-done | bytes 262176 | tf_op jit(solution)/shard_map/ppermute | solution.py:115
  742.6 7.8 fusion.20
  750.4 7.7 fusion.26
  760.4 8.2 fusion.4
  772.6 9.7 %fusion.5 = f32[512,2048]{1,0:T(8,128)} fusion(bf16[2048,2048]{1,0:T(8,128)(2,1)S(1)} %bitcast.317, f32[2048,512]{1,0:T(8,128)} %fusion.18, f32[2048,512]{1,0:T(8,128)} %fusion.14), kind=kOutput, calls=%fused_computation.25 | convolution fusion | flops 4301258752 | bytes 20971520 | tf_op jit(solution)/shard_map/dot_general | solution.py:54
  782.3 6.9 reshape.577
  807.9 18.9 %collective-permute-done.24 = bf16[4,512,256]{2,1,0:T(8,128)(2,1)S(1)} collective-permute-done((bf16[4,512,256]{2,1,0:T(8,128)(2,1)S(1)}, bf16[4,512,256]{2,1,0:T(8,128)(2,1)S(1)}, u32[]{:S(2)}, u32[]{:S(2)}) %collective-permute-start.24) | collective-permute-done | bytes 1048608 | tf_op jit(solution)/shard_map/ppermute | solution.py:115
  834.6 14.9 %collective-permute-done.22 = bf16[256,512]{1,0:T(8,128)(2,1)S(1)} collective-permute-done((bf16[256,512]{1,0:T(8,128)(2,1)S(1)}, bf16[256,512]{1,0:T(8,128)(2,1)S(1)}, u32[]{:S(2)}, u32[]{:S(2)}) %collective-permute-start.22) | collective-permute-done | bytes 262176 | tf_op jit(solution)/shard_map/ppermute | solution.py:115
  849.5 15.1 %collective-permute-done.23 = bf16[256,512]{1,0:T(8,128)(2,1)S(1)} collective-permute-done((bf16[256,512]{1,0:T(8,128)(2,1)S(1)}, bf16[256,512]{1,0:T(8,128)(2,1)S(1)}, u32[]{:S(2)}, u32[]{:S(2)}) %collective-permute-start.23) | collective-permute-done | bytes 262176 | tf_op jit(solution)/shard_map/ppermute | solution.py:115
  869.3 6.6 collective-permute-done.27
  (326 shorter events, 282.1 us)
Async XLA Ops:
  7.9 95.1 %reduce-scatter.5.cloned.1.call-start = ((), (), s32[]{:S(2)}) async-start(), calls=%async_computation.5 | async-start | bytes 2621440 | tf_op jit(solution)/shard_map/reduce_scatter | solution.py:210
  70.2 59.4 %all-gather.11.cloned.1.call-start = ((), (), s32[]{:S(2)}) async-start(), calls=%async_computation.6 | async-start | bytes 2621440 | tf_op jit(solution)/shard_map/all_gather | solution.py:220
  106.4 82.9 %reduce-scatter.7.cloned.1.call-start = ((), (), s32[]{:S(2)}) async-start(), calls=%async_computation.7 | async-start | bytes 2621440 | tf_op jit(solution)/shard_map/reduce_scatter | solution.py:234
  158.1 59.3 %all-gather.13.cloned.1.call-start = ((), (), s32[]{:S(2)}) async-start(), calls=%async_computation.8 | async-start | bytes 2621440 | tf_op jit(solution)/shard_map/all_gather | solution.py:246
  194.2 87.4 %reduce-scatter.9.cloned.1.call-start = ((), (), s32[]{:S(2)}) async-start(), calls=%async_computation.9 | async-start | bytes 2621440 | tf_op jit(solution)/shard_map/reduce_scatter | solution.py:273
  250.5 77.5 %all-gather.17.cloned.1.call-start = ((), (), s32[]{:S(2)}) async-start(), calls=%async_computation.12 | async-start | bytes 2621440 | tf_op jit(solution)/shard_map/all_gather | solution.py:226
  251.2 102.6 %all-gather.15.cloned.1.call-start = ((), (), s32[]{:S(2)}) async-start(), calls=%async_computation.10 | async-start | bytes 2621440 | tf_op jit(solution)/shard_map/all_gather | solution.py:280
  286.1 113.6 %all-gather.21.cloned.1.call-start = ((), (), s32[]{:S(2)}) async-start(), calls=%async_computation.14 | async-start | bytes 2621440 | tf_op jit(solution)/shard_map/all_gather | solution.py:226
  286.9 173.7 %all-gather.19.cloned.1.call-start = ((), (), s32[]{:S(2)}) async-start(), calls=%async_computation.13 | async-start | bytes 10485760 | tf_op jit(solution)/shard_map/all_gather | solution.py:227
  328.0 412.5 %reduce-scatter.11.cloned.1.call-start = ((), (), s32[]{:S(2)}) async-start(), calls=%async_computation.11 | async-start | bytes 2621440 | tf_op jit(solution)/shard_map/reduce_scatter | solution.py:307
  395.6 347.0 %all-gather.23.cloned.1.call-start = ((), (), s32[]{:S(2)}) async-start(), calls=%async_computation.15 | async-start | bytes 10485760 | tf_op jit(solution)/shard_map/all_gather | solution.py:227
  500.9 147.4 %collective-permute-start = (bf16[4,256,512]{2,1,0:T(8,128)(2,1)}, bf16[4,256,512]{2,1,0:T(8,128)(2,1)}, u32[]{:S(2)}, u32[]{:S(2)}) collective-permute-start(bf16[4,256,512]{2,1,0:T(8,128)(2,1)} %bitcast.298), channel_id=1, source_target_pairs={{0,4},{4,0},{8,12},{12,8},{16,20},{20,16},{24,28},{28,24},{1,5},{5... | collective-permute-start | bytes 3145736 | tf_op jit(solution)/shard_map/ppermute | solution.py:115
  523.5 130.4 %collective-permute-start.4 = (bf16[4,256,512]{2,1,0:T(8,128)(2,1)}, bf16[4,256,512]{2,1,0:T(8,128)(2,1)}, u32[]{:S(2)}, u32[]{:S(2)}) collective-permute-start(bf16[4,256,512]{2,1,0:T(8,128)(2,1)} %bitcast.297), channel_id=1, source_target_pairs={{0,4},{4,0},{8,12},{12,8},{16,20},{20,16},{24,28},{28,24},{1,5},{5... | collective-permute-start | bytes 3145736 | tf_op jit(solution)/shard_map/ppermute | solution.py:115
  542.2 113.6 %collective-permute-start.8 = (bf16[4,256,512]{2,1,0:T(8,128)(2,1)}, bf16[4,256,512]{2,1,0:T(8,128)(2,1)}, u32[]{:S(2)}, u32[]{:S(2)}) collective-permute-start(bf16[4,256,512]{2,1,0:T(8,128)(2,1)} %bitcast.296), channel_id=1, source_target_pairs={{0,4},{4,0},{8,12},{12,8},{16,20},{20,16},{24,28},{28,24},{1,5},{5... | collective-permute-start | bytes 3145736 | tf_op jit(solution)/shard_map/ppermute | solution.py:115
  548.5 109.2 %collective-permute-start.12 = (bf16[4,512,256]{2,1,0:T(8,128)(2,1)}, bf16[4,512,256]{2,1,0:T(8,128)(2,1)}, u32[]{:S(2)}, u32[]{:S(2)}) collective-permute-start(bf16[4,512,256]{2,1,0:T(8,128)(2,1)} %fusion.56), channel_id=1, source_target_pairs={{0,4},{4,0},{8,12},{12,8},{16,20},{20,16},{24,28},{28,24},{1,5},{5... | collective-permute-start | bytes 3145736 | tf_op jit(solution)/shard_map/ppermute | solution.py:115
  651.0 31.7 %collective-permute-start.2 = (bf16[256,512]{1,0:T(8,128)(2,1)S(1)}, bf16[256,512]{1,0:T(8,128)(2,1)S(1)}, u32[]{:S(2)}, u32[]{:S(2)}) collective-permute-start(bf16[256,512]{1,0:T(8,128)(2,1)S(1)} %get-tuple-element.70), channel_id=1, source_target_pairs={{0,16},{4,20},{8,24},{12,28},{16,0},{20,4},{24,8},{28,12},{1,17},{... | collective-permute-start | bytes 786440 | tf_op jit(solution)/shard_map/ppermute | solution.py:115
  655.7 46.2 %collective-permute-start.7 = (bf16[256,512]{1,0:T(8,128)(2,1)S(1)}, bf16[256,512]{1,0:T(8,128)(2,1)S(1)}, u32[]{:S(2)}, u32[]{:S(2)}) collective-permute-start(bf16[256,512]{1,0:T(8,128)(2,1)S(1)} %get-tuple-element.66), channel_id=1, source_target_pairs={{0,24},{4,28},{8,16},{12,20},{16,8},{20,12},{24,0},{28,4},{1,25},{... | collective-permute-start | bytes 786440 | tf_op jit(solution)/shard_map/ppermute | solution.py:115
  657.8 48.1 %collective-permute-start.6 = (bf16[256,512]{1,0:T(8,128)(2,1)S(1)}, bf16[256,512]{1,0:T(8,128)(2,1)S(1)}, u32[]{:S(2)}, u32[]{:S(2)}) collective-permute-start(bf16[256,512]{1,0:T(8,128)(2,1)S(1)} %get-tuple-element.67), channel_id=1, source_target_pairs={{0,16},{4,20},{8,24},{12,28},{16,0},{20,4},{24,8},{28,12},{1,17},{... | collective-permute-start | bytes 786440 | tf_op jit(solution)/shard_map/ppermute | solution.py:115
  668.2 38.7 %collective-permute-start.5 = (bf16[256,512]{1,0:T(8,128)(2,1)S(1)}, bf16[256,512]{1,0:T(8,128)(2,1)S(1)}, u32[]{:S(2)}, u32[]{:S(2)}) collective-permute-start(bf16[256,512]{1,0:T(8,128)(2,1)S(1)} %get-tuple-element.65), channel_id=1, source_target_pairs={{0,8},{4,12},{8,0},{12,4},{16,24},{20,28},{24,16},{28,20},{1,9},{5... | collective-permute-start | bytes 786440 | tf_op jit(solution)/shard_map/ppermute | solution.py:115
  682.7 41.8 %collective-permute-start.11 = (bf16[256,512]{1,0:T(8,128)(2,1)S(1)}, bf16[256,512]{1,0:T(8,128)(2,1)S(1)}, u32[]{:S(2)}, u32[]{:S(2)}) collective-permute-start(bf16[256,512]{1,0:T(8,128)(2,1)S(1)} %get-tuple-element.63), channel_id=1, source_target_pairs={{0,24},{4,28},{8,16},{12,20},{16,8},{20,12},{24,0},{28,4},{1,25},{... | collective-permute-start | bytes 786440 | tf_op jit(solution)/shard_map/ppermute | solution.py:115
  683.8 44.5 %collective-permute-start.10 = (bf16[256,512]{1,0:T(8,128)(2,1)S(1)}, bf16[256,512]{1,0:T(8,128)(2,1)S(1)}, u32[]{:S(2)}, u32[]{:S(2)}) collective-permute-start(bf16[256,512]{1,0:T(8,128)(2,1)S(1)} %get-tuple-element.64), channel_id=1, source_target_pairs={{0,16},{4,20},{8,24},{12,28},{16,0},{20,4},{24,8},{28,12},{1,17},{... | collective-permute-start | bytes 786440 | tf_op jit(solution)/shard_map/ppermute | solution.py:115
  706.9 32.7 %collective-permute-start.14 = (bf16[512,256]{1,0:T(8,128)(2,1)S(1)}, bf16[512,256]{1,0:T(8,128)(2,1)S(1)}, u32[]{:S(2)}, u32[]{:S(2)}) collective-permute-start(bf16[512,256]{1,0:T(8,128)(2,1)S(1)} %get-tuple-element.61), channel_id=1, source_target_pairs={{0,16},{4,20},{8,24},{12,28},{16,0},{20,4},{24,8},{28,12},{1,17},{... | collective-permute-start | bytes 786440 | tf_op jit(solution)/shard_map/ppermute | solution.py:115
  759.2 37.0 %collective-permute-start.16 = (bf16[4,256,512]{2,1,0:T(8,128)(2,1)}, bf16[4,256,512]{2,1,0:T(8,128)(2,1)}, u32[]{:S(2)}, u32[]{:S(2)}) collective-permute-start(bf16[4,256,512]{2,1,0:T(8,128)(2,1)} %fusion.58), channel_id=1, source_target_pairs={{0,4},{4,0},{8,12},{12,8},{16,20},{20,16},{24,28},{28,24},{1,5},{5... | collective-permute-start | bytes 3145736 | tf_op jit(solution)/shard_map/ppermute | solution.py:115
  771.7 32.5 %collective-permute-start.20 = (bf16[4,256,512]{2,1,0:T(8,128)(2,1)}, bf16[4,256,512]{2,1,0:T(8,128)(2,1)S(1)}, u32[]{:S(2)}, u32[]{:S(2)}) collective-permute-start(bf16[4,256,512]{2,1,0:T(8,128)(2,1)} %fusion.59), channel_id=1, source_target_pairs={{0,4},{4,0},{8,12},{12,8},{16,20},{20,16},{24,28},{28,24},{1,5},{5... | collective-permute-start | bytes 3145736 | tf_op jit(solution)/shard_map/ppermute | solution.py:115
  793.8 32.9 %collective-permute-start.24 = (bf16[4,512,256]{2,1,0:T(8,128)(2,1)S(1)}, bf16[4,512,256]{2,1,0:T(8,128)(2,1)S(1)}, u32[]{:S(2)}, u32[]{:S(2)}) collective-permute-start(bf16[4,512,256]{2,1,0:T(8,128)(2,1)S(1)} %bitcast.299), channel_id=1, source_target_pairs={{0,4},{4,0},{8,12},{12,8},{16,20},{20,16},{24,28},{28,24},{1,5},{5... | collective-permute-start | bytes 3145736 | tf_op jit(solution)/shard_map/ppermute | solution.py:115
  798.2 32.3 %collective-permute-start.17 = (bf16[256,512]{1,0:T(8,128)(2,1)S(1)}, bf16[256,512]{1,0:T(8,128)(2,1)S(1)}, u32[]{:S(2)}, u32[]{:S(2)}) collective-permute-start(bf16[256,512]{1,0:T(8,128)(2,1)S(1)} %get-tuple-element.57), channel_id=1, source_target_pairs={{0,8},{4,12},{8,0},{12,4},{16,24},{20,28},{24,16},{28,20},{1,9},{5... | collective-permute-start | bytes 786440 | tf_op jit(solution)/shard_map/ppermute | solution.py:115
  801.3 30.4 %collective-permute-start.18 = (bf16[256,512]{1,0:T(8,128)(2,1)S(1)}, bf16[256,512]{1,0:T(8,128)(2,1)S(1)}, u32[]{:S(2)}, u32[]{:S(2)}) collective-permute-start(bf16[256,512]{1,0:T(8,128)(2,1)S(1)} %get-tuple-element.56), channel_id=1, source_target_pairs={{0,16},{4,20},{8,24},{12,28},{16,0},{20,4},{24,8},{28,12},{1,17},{... | collective-permute-start | bytes 786440 | tf_op jit(solution)/shard_map/ppermute | solution.py:115
  801.4 30.4 %collective-permute-start.19 = (bf16[256,512]{1,0:T(8,128)(2,1)S(1)}, bf16[256,512]{1,0:T(8,128)(2,1)S(1)}, u32[]{:S(2)}, u32[]{:S(2)}) collective-permute-start(bf16[256,512]{1,0:T(8,128)(2,1)S(1)} %get-tuple-element.55), channel_id=1, source_target_pairs={{0,24},{4,28},{8,16},{12,20},{16,8},{20,12},{24,0},{28,4},{1,25},{... | collective-permute-start | bytes 786440 | tf_op jit(solution)/shard_map/ppermute | solution.py:115
  830.5 34.2 %collective-permute-start.23 = (bf16[256,512]{1,0:T(8,128)(2,1)S(1)}, bf16[256,512]{1,0:T(8,128)(2,1)S(1)}, u32[]{:S(2)}, u32[]{:S(2)}) collective-permute-start(bf16[256,512]{1,0:T(8,128)(2,1)S(1)} %get-tuple-element.47), channel_id=1, source_target_pairs={{0,24},{4,28},{8,16},{12,20},{16,8},{20,12},{24,0},{28,4},{1,25},{... | collective-permute-start | bytes 786440 | tf_op jit(solution)/shard_map/ppermute | solution.py:115
  831.7 33.0 %collective-permute-start.25 = (bf16[512,256]{1,0:T(8,128)(2,1)S(1)}, bf16[512,256]{1,0:T(8,128)(2,1)S(1)}, u32[]{:S(2)}, u32[]{:S(2)}) collective-permute-start(bf16[512,256]{1,0:T(8,128)(2,1)S(1)} %get-tuple-element.41), channel_id=1, source_target_pairs={{0,8},{4,12},{8,0},{12,4},{16,24},{20,28},{24,16},{28,20},{1,9},{5... | collective-permute-start | bytes 786440 | tf_op jit(solution)/shard_map/ppermute | solution.py:115
  831.9 37.3 %collective-permute-start.26 = (bf16[512,256]{1,0:T(8,128)(2,1)S(1)}, bf16[512,256]{1,0:T(8,128)(2,1)S(1)}, u32[]{:S(2)}, u32[]{:S(2)}) collective-permute-start(bf16[512,256]{1,0:T(8,128)(2,1)S(1)} %get-tuple-element.40), channel_id=1, source_target_pairs={{0,16},{4,20},{8,24},{12,28},{16,0},{20,4},{24,8},{28,12},{1,17},{... | collective-permute-start | bytes 786440 | tf_op jit(solution)/shard_map/ppermute | solution.py:115
  833.4 42.5 %collective-permute-start.27 = (bf16[512,256]{1,0:T(8,128)(2,1)S(1)}, bf16[512,256]{1,0:T(8,128)(2,1)S(1)}, u32[]{:S(2)}, u32[]{:S(2)}) collective-permute-start(bf16[512,256]{1,0:T(8,128)(2,1)S(1)} %get-tuple-element.39), channel_id=1, source_target_pairs={{0,24},{4,28},{8,16},{12,20},{16,8},{20,12},{24,0},{28,4},{1,25},{... | collective-permute-start | bytes 786440 | tf_op jit(solution)/shard_map/ppermute | solution.py:115
  (69 other events, 836.6 us)
Sparse Core Ops, SparseCore 0:
  9.6 24.1 all-gather.8
  70.3 32.6 reduce-scatter.4
  106.5 23.0 all-gather.10
  158.2 31.0 reduce-scatter.6
  194.4 22.9 all-gather.12
  250.6 31.0 reduce-scatter.8
  283.9 44.0 all-gather.16
  330.2 23.5 all-gather.14
  356.0 43.6 all-gather.20
  401.2 59.2 all-gather.18
  463.8 30.9 reduce-scatter.10
  496.2 58.7 all-gather.22
where the time goes:
time: 898 us; the launch traced here: 888 us
  waiting for transfers between devices  420 us (47%)
  matrix products  149 us (17%)
  local copies, waits for them, and re-layouts  124 us (14%)
  blocking collectives  82.2 us (9%)
  other arithmetic  56.8 us (6%)
  starting transfers between devices  38.8 us (4%)
  between operations  15.9 us (2%)
    ppermute x28, waiting for transfers between devices, swap(): return lax.ppermute(value, 'dp', [(d, d ^ shift) for d in range(size)])  125 us
    psum x1, blocking collectives, body(): gain_total = lax.psum(gain_stack, ('dp', 'tensor'))  71.2 us
    all_gather x2, waiting for transfers between devices, gather_group(): return lax.all_gather(part, 'tensor', axis=0, tiled=True)  60.7 us
    dot_general x8, matrix products, times_t(): lax.dot_general(left_mat, right_mat, (((1,), (1,)), ((), ())), preferred_...  49.7 us
    all_gather x2, waiting for transfers between devices, gather_group(): lax.all_gather(shard, 'dp', axis=0, tiled=True, axis_index_groups=groups)  45.1 us
    another operation x12, local copies, waits for them, and re-layouts  42.2 us
    ppermute x28, starting transfers between devices, swap(): return lax.ppermute(value, 'dp', [(d, d ^ shift) for d in range(size)])  37.8 us
    dot_general x7, matrix products, t_times(): lax.dot_general(left_mat, right_mat, (((0,), (0,)), ((), ())), preferred_...  36.6 us
  transfers between devices with their start and end apart: 40, of which 24 were waited for; matrix products, arithmetic and copies ran while one was open for 23% of the time, Pallas kernels for 0%

commit v1 on v0

--- a/solution.py
+++ b/solution.py
@@ -320,7 +320,7 @@
     q_full = lax.dynamic_update_slice(zero_row, grad_gain_query_part, (tensor_start,))
     k_full = lax.dynamic_update_slice(zero_row, grad_gain_key_part, (tensor_start,))
     gain_stack = jnp.stack([q_full, k_full, grad_gain_attn_part, grad_gain_mlp_part])
-    gain_total = lax.psum(gain_stack, ("dp", "tensor"))
+    gain_total = jnp.sum(lax.all_gather(gain_stack, ("dp", "tensor")), axis=0)
     grad_gain_query = lax.dynamic_slice(gain_total[0], (tensor_start,), (local_width,))
     grad_gain_key = lax.dynamic_slice(gain_total[1], (tensor_start,), (local_width,))
     summed = (

time: 898 us -> 835 us (0.930)
  blocking collectives: 82.2 us -> 10.8 us
  waiting for transfers between devices: 420 us -> 431 us
    psum x1 -> x0, blocking collectives: 71.2 us -> none  [body(): gain_total = lax.psum(gain_stack, ('dp', 'tensor'))]
    ppermute x28, waiting for transfers between devices: 125 us -> 138 us  [swap(): return lax.ppermute(value, 'dp', [(d, d ^ shift) for d in range(size)])]
    unnamed x130 -> x126, local copies, waits for them, and re-layouts: 34.7 us -> 35.8 us
  transfers between devices with their start and end apart: 40 -> 41, of which waited for: 24 -> 23; matrix products, arithmetic and copies ran while one was open for 23% -> 25% of each run, Pallas kernels for 0% -> 0%
where the time goes in v1:
time: 835 us; the launch traced here: 822 us
  waiting for transfers between devices  431 us (52%)
  matrix products  153 us (18%)
  local copies, waits for them, and re-layouts  125 us (15%)
  other arithmetic  56.6 us (7%)
  starting transfers between devices  30.4 us (4%)
  between operations  15.6 us (2%)
  blocking collectives  10.8 us (1%)
    ppermute x28, waiting for transfers between devices, swap(): return lax.ppermute(value, 'dp', [(d, d ^ shift) for d in range(size)])  138 us
    all_gather x2, waiting for transfers between devices, gather_group(): return lax.all_gather(part, 'tensor', axis=0, tiled=True)  60.7 us
    dot_general x8, matrix products, times_t(): lax.dot_general(left_mat, right_mat, (((1,), (1,)), ((), ())), preferred_...  49.7 us
    all_gather x2, waiting for transfers between devices, gather_group(): lax.all_gather(shard, 'dp', axis=0, tiled=True, axis_index_groups=groups)  43.1 us
    another operation x12, local copies, waits for them, and re-layouts  41.7 us
    dot_general x7, matrix products, t_times(): lax.dot_general(left_mat, right_mat, (((0,), (0,)), ((), ())), preferred_...  38.6 us
    unnamed x126, local copies, waits for them, and re-layouts  35.8 us
    reduce_scatter x1, waiting for transfers between devices, body(): lax.psum_scatter(jnp.dot(mixed_low, w_out, preferred_element_type=jnp.flo...  32.8 us
  transfers between devices with their start and end apart: 41, of which 23 were waited for; matrix products, arithmetic and copies ran while one was open for 25% of the time, Pallas kernels for 0%

profile of v1, /device:TPU:9, one launch (start us, length us, event | category | flops | bytes accessed | tf_op | source)
XLA Modules:
  0.0 822.3 jit_solution(2138460820404268290)
XLA Ops:
  12.2 21.6 %all-gather.12.cloned.1.call-done = bf16[512,2048]{1,0:T(8,128)(2,1)} async-done(((bf16[128,2048]{1,0:T(8,128)(2,1)}), bf16[512,2048]{1,0:T(8,128)(2,1)}) %all-gather.12.cloned.1.call-update) | async-done | bytes 2097168 | tf_op jit(solution)/shard_map/all_gather | solution.py:186
  70.3 32.8 %reduce-scatter.5.cloned.1.call-done = bf16[128,2048]{1,0:T(8,128)(2,1)} async-done(((bf16[512,2048]{1,0:T(8,128)(2,1)}), bf16[128,2048]{1,0:T(8,128)(2,1)}) %reduce-scatter.5.cloned.1.call-update) | async-done | bytes 524304 | tf_op jit(solution)/shard_map/reduce_scatter | solution.py:210
  106.9 22.8 %all-gather.14.cloned.1.call-done = bf16[512,2048]{1,0:T(8,128)(2,1)} async-done(((bf16[128,2048]{1,0:T(8,128)(2,1)}), bf16[512,2048]{1,0:T(8,128)(2,1)}) %all-gather.14.cloned.1.call-update) | async-done | bytes 2097168 | tf_op jit(solution)/shard_map/all_gather | solution.py:220
  129.6 8.6 %fusion.92 = f32[512,2048]{1,0:T(8,128)S(1)} fusion(bf16[512,2048]{1,0:T(8,128)(2,1)} %all-gather.14.cloned.1.call-done, bf16[2048,2048]{1,0:T(8,128)(2,1)} %param.20), kind=kOutput, calls=%fused_computation.245 | convolution fusion | flops 4294967296 | bytes 14680064 | tf_op jit(solution)/shard_map/dot_general | solution.py:230
  138.2 8.4 %fusion.93 = f32[512,2048]{1,0:T(8,128)S(1)} fusion(bf16[512,2048]{1,0:T(8,128)(2,1)S(1)} %copy-done.50, bf16[2048,2048]{1,0:T(8,128)(2,1)} %param.21), kind=kOutput, calls=%fused_computation.246 | convolution fusion | flops 4294967296 | bytes 14680064 | tf_op jit(solution)/shard_map/dot_general | solution.py:231
  148.7 9.5 %convolution_convert_fusion = bf16[512,2048]{1,0:T(8,128)(2,1)} fusion(bf16[2048,2048]{1,0:T(8,128)(2,1)} %param.22, f32[512,2048]{1,0:T(8,128)S(1)} %fusion.93, f32[512,2048]{1,0:T(8,128)S(1)} %fusion.92), kind=kOutput, calls=%fused_computation.21 | convolution fusion | flops 4302307328 | bytes 18874368 | tf_op jit(solution)/shard_map/dot_general | solution.py:235
  158.2 31.1 %reduce-scatter.7.cloned.1.call-done = bf16[128,2048]{1,0:T(8,128)(2,1)} async-done(((bf16[512,2048]{1,0:T(8,128)(2,1)}), bf16[128,2048]{1,0:T(8,128)(2,1)}) %reduce-scatter.7.cloned.1.call-update) | async-done | bytes 524304 | tf_op jit(solution)/shard_map/reduce_scatter | solution.py:234
  194.3 23.1 %all-gather.16.cloned.1.call-done = bf16[512,2048]{1,0:T(8,128)(2,1)} async-done(((bf16[128,2048]{1,0:T(8,128)(2,1)}), bf16[512,2048]{1,0:T(8,128)(2,1)}) %all-gather.16.cloned.1.call-update) | async-done | bytes 2097168 | tf_op jit(solution)/shard_map/all_gather | solution.py:246
  217.5 7.6 fusion.94
  225.1 13.6 %fusion.25 = f32[512,2048]{1,0:T(8,128)} fusion(bf16[2048,2048]{1,0:T(8,128)(2,1)} %param.20, f32[512,2048]{1,0:T(8,128)} %copy-done.51, f32[512,2048]{1,0:T(8,128)S(1)} %fusion.94, f32[512,2048]{1,0:T(8,128)} %copy-done.52), kind=kOutput, calls=%fused_computation.56 | convolution fusion | flops 4305453056 | bytes 25165824 | tf_op jit(solution)/shard_map/dot_general | solution.py:48
  238.7 11.8 %add_convert_fusion.1 = bf16[512,2048]{1,0:T(8,128)(2,1)} fusion(f32[512,2048]{1,0:T(8,128)} %fusion.25, bf16[2048,2048]{1,0:T(8,128)(2,1)} %param.21, f32[512,2048]{1,0:T(8,128)S(1)} %fusion.94, f32[512,2048]{1,0:T(8,128)} %copy-done.51), kind=kOutput, calls=%fused_computation.8 | convolution fusion | flops 4303355904 | bytes 23068672 | tf_op jit(solution)/shard_map/dot_general | solution.py:48
  251.3 30.4 %reduce-scatter.9.cloned.1.call-done = bf16[128,2048]{1,0:T(8,128)(2,1)} async-done(((bf16[512,2048]{1,0:T(8,128)(2,1)}), bf16[128,2048]{1,0:T(8,128)(2,1)}) %reduce-scatter.9.cloned.1.call-update) | async-done | bytes 524304 | tf_op jit(solution)/shard_map/reduce_scatter | solution.py:273
  287.0 41.1 %all-gather.20.cloned.1.call-done = bf16[512,2048]{1,0:T(8,128)(2,1)} async-done(((bf16[128,2048]{1,0:T(8,128)(2,1)}), bf16[512,2048]{1,0:T(8,128)(2,1)}) %all-gather.20.cloned.1.call-update) | async-done | bytes 2097168 | tf_op jit(solution)/shard_map/all_gather | solution.py:226
  328.3 25.5 %all-gather.18.cloned.1.call-done = bf16[512,2048]{1,0:T(8,128)(2,1)} async-done(((bf16[128,2048]{1,0:T(8,128)(2,1)}), bf16[512,2048]{1,0:T(8,128)(2,1)}) %all-gather.18.cloned.1.call-update) | async-done | bytes 2097168 | tf_op jit(solution)/shard_map/all_gather | solution.py:280
  399.9 60.7 %all-gather.22.cloned.1.call-done = bf16[2048,2048]{1,0:T(8,128)(2,1)} async-done(((bf16[512,2048]{1,0:T(8,128)(2,1)}), bf16[2048,2048]{1,0:T(8,128)(2,1)}) %all-gather.22.cloned.1.call-update) | async-done | bytes 8388624 | tf_op jit(solution)/shard_map/all_gather | solution.py:227
  460.6 10.6 %fusion.14 = f32[2048,512]{1,0:T(8,128)} fusion(bf16[2048,2048]{1,0:T(8,128)(2,1)} %all-gather.22.cloned.1.call-done, bf16[2048,2048]{1,0:T(8,128)(2,1)} %param.20, s32[]{:T(128)S(6)} %select_n.141), kind=kOutput, calls=%fused_computation.44 | convolution fusion | flops 4294967296 | bytes 14680068 | tf_op jit(solution)/shard_map/dot_general | solution.py:257
  471.3 8.3 %fusion.18 = f32[2048,512]{1,0:T(8,128)} fusion(bf16[2048,2048]{1,0:T(8,128)(2,1)S(1)} %copy-done.48, bf16[2048,2048]{1,0:T(8,128)(2,1)} %param.21, s32[]{:T(128)S(6)} %select_n.141), kind=kOutput, calls=%fused_computation.48 | convolution fusion | flops 4294967296 | bytes 14680068 | tf_op jit(solution)/shard_map/dot_general | solution.py:258
  482.8 6.6 reshape.572
  526.7 6.8 reshape.574
  584.1 8.7 %collective-permute-done.8 = bf16[4,256,512]{2,1,0:T(8,128)(2,1)} collective-permute-done((bf16[4,256,512]{2,1,0:T(8,128)(2,1)}, bf16[4,256,512]{2,1,0:T(8,128)(2,1)}, u32[]{:S(2)}, u32[]{:S(2)}) %collective-permute-start.8) | collective-permute-done | bytes 1048608 | tf_op jit(solution)/shard_map/ppermute | solution.py:115
  595.7 19.5 %collective-permute-done.12 = bf16[4,512,256]{2,1,0:T(8,128)(2,1)S(1)} collective-permute-done((bf16[4,512,256]{2,1,0:T(8,128)(2,1)S(1)}, bf16[4,512,256]{2,1,0:T(8,128)(2,1)S(1)}, u32[]{:S(2)}, u32[]{:S(2)}) %collective-permute-start.12) | collective-permute-done | bytes 1048608 | tf_op jit(solution)/shard_map/ppermute | solution.py:115
  622.5 8.0 collective-permute-done.6
  634.0 13.2 %collective-permute-done.11 = bf16[256,512]{1,0:T(8,128)(2,1)S(1)} collective-permute-done((bf16[256,512]{1,0:T(8,128)(2,1)S(1)}, bf16[256,512]{1,0:T(8,128)(2,1)S(1)}, u32[]{:S(2)}, u32[]{:S(2)}) %collective-permute-start.11) | collective-permute-done | bytes 262176 | tf_op jit(solution)/shard_map/ppermute | solution.py:115
  648.2 14.6 %collective-permute-done.10 = bf16[256,512]{1,0:T(8,128)(2,1)S(1)} collective-permute-done((bf16[256,512]{1,0:T(8,128)(2,1)S(1)}, bf16[256,512]{1,0:T(8,128)(2,1)S(1)}, u32[]{:S(2)}, u32[]{:S(2)}) %collective-permute-start.10) | collective-permute-done | bytes 262176 | tf_op jit(solution)/shard_map/ppermute | solution.py:115
  680.2 7.8 fusion.20
  688.0 7.7 fusion.26
  697.6 8.4 %fusion.4 = f32[2048,512]{1,0:T(8,128)S(1)} fusion(bf16[2048,2048]{1,0:T(8,128)(2,1)S(1)} %bitcast.317, f32[2048,512]{1,0:T(8,128)S(1)} %fusion.20, f32[2048,512]{1,0:T(8,128)} %fusion.14), kind=kOutput, calls=%fused_computation.24 | convolution fusion | flops 4301258752 | bytes 20971520 | tf_op jit(solution)/shard_map/dot_general | solution.py:54
  710.0 9.8 %fusion.5 = f32[512,2048]{1,0:T(8,128)} fusion(bf16[2048,2048]{1,0:T(8,128)(2,1)S(1)} %bitcast.319, f32[2048,512]{1,0:T(8,128)} %fusion.18, f32[2048,512]{1,0:T(8,128)} %fusion.14), kind=kOutput, calls=%fused_computation.25 | convolution fusion | flops 4301258752 | bytes 20971520 | tf_op jit(solution)/shard_map/dot_general | solution.py:54
  719.8 6.9 reshape.577
  744.3 21.8 %collective-permute-done.24 = bf16[4,512,256]{2,1,0:T(8,128)(2,1)S(1)} collective-permute-done((bf16[4,512,256]{2,1,0:T(8,128)(2,1)S(1)}, bf16[4,512,256]{2,1,0:T(8,128)(2,1)S(1)}, u32[]{:S(2)}, u32[]{:S(2)}) %collective-permute-start.24) | collective-permute-done | bytes 1048608 | tf_op jit(solution)/shard_map/ppermute | solution.py:115
  773.0 10.5 %collective-permute-done.22 = bf16[256,512]{1,0:T(8,128)(2,1)S(1)} collective-permute-done((bf16[256,512]{1,0:T(8,128)(2,1)S(1)}, bf16[256,512]{1,0:T(8,128)(2,1)S(1)}, u32[]{:S(2)}, u32[]{:S(2)}) %collective-permute-start.22) | collective-permute-done | bytes 262176 | tf_op jit(solution)/shard_map/ppermute | solution.py:115
  783.6 15.7 %collective-permute-done.23 = bf16[256,512]{1,0:T(8,128)(2,1)S(1)} collective-permute-done((bf16[256,512]{1,0:T(8,128)(2,1)S(1)}, bf16[256,512]{1,0:T(8,128)(2,1)S(1)}, u32[]{:S(2)}, u32[]{:S(2)}) %collective-permute-start.23) | collective-permute-done | bytes 262176 | tf_op jit(solution)/shard_map/ppermute | solution.py:115
  (325 shorter events, 273.2 us)
Async XLA Ops:
  7.9 95.2 %reduce-scatter.5.cloned.1.call-start = ((), (), s32[]{:S(2)}) async-start(), calls=%async_computation.5 | async-start | bytes 2621440 | tf_op jit(solution)/shard_map/reduce_scatter | solution.py:210
  70.2 59.4 %all-gather.14.cloned.1.call-start = ((), (), s32[]{:S(2)}) async-start(), calls=%async_computation.6 | async-start | bytes 2621440 | tf_op jit(solution)/shard_map/all_gather | solution.py:220
  106.5 82.9 %reduce-scatter.7.cloned.1.call-start = ((), (), s32[]{:S(2)}) async-start(), calls=%async_computation.7 | async-start | bytes 2621440 | tf_op jit(solution)/shard_map/reduce_scatter | solution.py:234
  158.2 59.3 %all-gather.16.cloned.1.call-start = ((), (), s32[]{:S(2)}) async-start(), calls=%async_computation.8 | async-start | bytes 2621440 | tf_op jit(solution)/shard_map/all_gather | solution.py:246
  194.3 87.4 %reduce-scatter.9.cloned.1.call-start = ((), (), s32[]{:S(2)}) async-start(), calls=%async_computation.9 | async-start | bytes 2621440 | tf_op jit(solution)/shard_map/reduce_scatter | solution.py:273
  250.5 77.5 %all-gather.20.cloned.1.call-start = ((), (), s32[]{:S(2)}) async-start(), calls=%async_computation.12 | async-start | bytes 2621440 | tf_op jit(solution)/shard_map/all_gather | solution.py:226
  251.3 102.6 %all-gather.18.cloned.1.call-start = ((), (), s32[]{:S(2)}) async-start(), calls=%async_computation.10 | async-start | bytes 2621440 | tf_op jit(solution)/shard_map/all_gather | solution.py:280
  286.2 113.6 %all-gather.24.cloned.1.call-start = ((), (), s32[]{:S(2)}) async-start(), calls=%async_computation.14 | async-start | bytes 2621440 | tf_op jit(solution)/shard_map/all_gather | solution.py:226
  286.9 173.7 %all-gather.22.cloned.1.call-start = ((), (), s32[]{:S(2)}) async-start(), calls=%async_computation.13 | async-start | bytes 10485760 | tf_op jit(solution)/shard_map/all_gather | solution.py:227
  328.1 346.8 %all-gather.28.cloned.1.call-start = ((), (), s32[]{:S(2)}) async-start(), calls=%async_computation.16 | async-start | bytes 1081344 | tf_op jit(solution)/shard_map/all_gather | solution.py:323
  386.2 291.9 %reduce-scatter.11.cloned.1.call-start = ((), (), s32[]{:S(2)}) async-start(), calls=%async_computation.11 | async-start | bytes 2621440 | tf_op jit(solution)/shard_map/reduce_scatter | solution.py:307
  397.7 282.5 %all-gather.26.cloned.1.call-start = ((), (), s32[]{:S(2)}) async-start(), calls=%async_computation.15 | async-start | bytes 10485760 | tf_op jit(solution)/shard_map/all_gather | solution.py:227
  500.7 76.6 %collective-permute-start = (bf16[4,256,512]{2,1,0:T(8,128)(2,1)}, bf16[4,256,512]{2,1,0:T(8,128)(2,1)}, u32[]{:S(2)}, u32[]{:S(2)}) collective-permute-start(bf16[4,256,512]{2,1,0:T(8,128)(2,1)} %bitcast.300), channel_id=1, source_target_pairs={{0,4},{4,0},{8,12},{12,8},{16,20},{20,16},{24,28},{28,24},{1,5},{5... | collective-permute-start | bytes 3145736 | tf_op jit(solution)/shard_map/ppermute | solution.py:115
  523.1 58.4 %collective-permute-start.4 = (bf16[4,256,512]{2,1,0:T(8,128)(2,1)}, bf16[4,256,512]{2,1,0:T(8,128)(2,1)}, u32[]{:S(2)}, u32[]{:S(2)}) collective-permute-start(bf16[4,256,512]{2,1,0:T(8,128)(2,1)} %bitcast.298), channel_id=1, source_target_pairs={{0,4},{4,0},{8,12},{12,8},{16,20},{20,16},{24,28},{28,24},{1,5},{5... | collective-permute-start | bytes 3145736 | tf_op jit(solution)/shard_map/ppermute | solution.py:115
  576.8 38.4 %collective-permute-start.12 = (bf16[4,512,256]{2,1,0:T(8,128)(2,1)S(1)}, bf16[4,512,256]{2,1,0:T(8,128)(2,1)S(1)}, u32[]{:S(2)}, u32[]{:S(2)}) collective-permute-start(bf16[4,512,256]{2,1,0:T(8,128)(2,1)S(1)} %fusion.56), channel_id=1, source_target_pairs={{0,4},{4,0},{8,12},{12,8},{16,20},{20,16},{24,28},{28,24},{1,5},{5... | collective-permute-start | bytes 3145736 | tf_op jit(solution)/shard_map/ppermute | solution.py:115
  579.0 38.7 %collective-permute-start.3 = (bf16[256,512]{1,0:T(8,128)(2,1)S(1)}, bf16[256,512]{1,0:T(8,128)(2,1)S(1)}, u32[]{:S(2)}, u32[]{:S(2)}) collective-permute-start(bf16[256,512]{1,0:T(8,128)(2,1)S(1)} %get-tuple-element.69), channel_id=1, source_target_pairs={{0,24},{4,28},{8,16},{12,20},{16,8},{20,12},{24,0},{28,4},{1,25},{... | collective-permute-start | bytes 786440 | tf_op jit(solution)/shard_map/ppermute | solution.py:115
  580.3 37.8 %collective-permute-start.2 = (bf16[256,512]{1,0:T(8,128)(2,1)S(1)}, bf16[256,512]{1,0:T(8,128)(2,1)S(1)}, u32[]{:S(2)}, u32[]{:S(2)}) collective-permute-start(bf16[256,512]{1,0:T(8,128)(2,1)S(1)} %get-tuple-element.70), channel_id=1, source_target_pairs={{0,16},{4,20},{8,24},{12,28},{16,0},{20,4},{24,8},{28,12},{1,17},{... | collective-permute-start | bytes 786440 | tf_op jit(solution)/shard_map/ppermute | solution.py:115
  581.5 36.9 %collective-permute-start.1 = (bf16[256,512]{1,0:T(8,128)(2,1)S(1)}, bf16[256,512]{1,0:T(8,128)(2,1)S(1)}, u32[]{:S(2)}, u32[]{:S(2)}) collective-permute-start(bf16[256,512]{1,0:T(8,128)(2,1)S(1)} %get-tuple-element.68), channel_id=1, source_target_pairs={{0,8},{4,12},{8,0},{12,4},{16,24},{20,28},{24,16},{28,20},{1,9},{5... | collective-permute-start | bytes 786440 | tf_op jit(solution)/shard_map/ppermute | solution.py:115
  618.4 44.4 %collective-permute-start.10 = (bf16[256,512]{1,0:T(8,128)(2,1)S(1)}, bf16[256,512]{1,0:T(8,128)(2,1)S(1)}, u32[]{:S(2)}, u32[]{:S(2)}) collective-permute-start(bf16[256,512]{1,0:T(8,128)(2,1)S(1)} %get-tuple-element.64), channel_id=1, source_target_pairs={{0,16},{4,20},{8,24},{12,28},{16,0},{20,4},{24,8},{28,12},{1,17},{... | collective-permute-start | bytes 786440 | tf_op jit(solution)/shard_map/ppermute | solution.py:115
  621.5 41.2 %collective-permute-start.9 = (bf16[256,512]{1,0:T(8,128)(2,1)S(1)}, bf16[256,512]{1,0:T(8,128)(2,1)S(1)}, u32[]{:S(2)}, u32[]{:S(2)}) collective-permute-start(bf16[256,512]{1,0:T(8,128)(2,1)S(1)} %get-tuple-element.62), channel_id=1, source_target_pairs={{0,8},{4,12},{8,0},{12,4},{16,24},{20,28},{24,16},{28,20},{1,9},{5... | collective-permute-start | bytes 786440 | tf_op jit(solution)/shard_map/ppermute | solution.py:115
  630.4 37.9 %collective-permute-start.15 = (bf16[512,256]{1,0:T(8,128)(2,1)S(1)}, bf16[512,256]{1,0:T(8,128)(2,1)S(1)}, u32[]{:S(2)}, u32[]{:S(2)}) collective-permute-start(bf16[512,256]{1,0:T(8,128)(2,1)S(1)} %get-tuple-element.60), channel_id=1, source_target_pairs={{0,24},{4,28},{8,16},{12,20},{16,8},{20,12},{24,0},{28,4},{1,25},{... | collective-permute-start | bytes 786440 | tf_op jit(solution)/shard_map/ppermute | solution.py:115
  630.4 43.6 %collective-permute-start.14 = (bf16[512,256]{1,0:T(8,128)(2,1)S(1)}, bf16[512,256]{1,0:T(8,128)(2,1)S(1)}, u32[]{:S(2)}, u32[]{:S(2)}) collective-permute-start(bf16[512,256]{1,0:T(8,128)(2,1)S(1)} %get-tuple-element.61), channel_id=1, source_target_pairs={{0,16},{4,20},{8,24},{12,28},{16,0},{20,4},{24,8},{28,12},{1,17},{... | collective-permute-start | bytes 786440 | tf_op jit(solution)/shard_map/ppermute | solution.py:115
  696.8 37.0 %collective-permute-start.16 = (bf16[4,256,512]{2,1,0:T(8,128)(2,1)}, bf16[4,256,512]{2,1,0:T(8,128)(2,1)}, u32[]{:S(2)}, u32[]{:S(2)}) collective-permute-start(bf16[4,256,512]{2,1,0:T(8,128)(2,1)} %fusion.58), channel_id=1, source_target_pairs={{0,4},{4,0},{8,12},{12,8},{16,20},{20,16},{24,28},{28,24},{1,5},{5... | collective-permute-start | bytes 3145736 | tf_op jit(solution)/shard_map/ppermute | solution.py:115
  709.2 34.5 %collective-permute-start.20 = (bf16[4,256,512]{2,1,0:T(8,128)(2,1)}, bf16[4,256,512]{2,1,0:T(8,128)(2,1)S(1)}, u32[]{:S(2)}, u32[]{:S(2)}) collective-permute-start(bf16[4,256,512]{2,1,0:T(8,128)(2,1)} %fusion.59), channel_id=1, source_target_pairs={{0,4},{4,0},{8,12},{12,8},{16,20},{20,16},{24,28},{28,24},{1,5},{5... | collective-permute-start | bytes 3145736 | tf_op jit(solution)/shard_map/ppermute | solution.py:115
  731.3 34.9 %collective-permute-start.24 = (bf16[4,512,256]{2,1,0:T(8,128)(2,1)S(1)}, bf16[4,512,256]{2,1,0:T(8,128)(2,1)S(1)}, u32[]{:S(2)}, u32[]{:S(2)}) collective-permute-start(bf16[4,512,256]{2,1,0:T(8,128)(2,1)S(1)} %bitcast.299), channel_id=1, source_target_pairs={{0,4},{4,0},{8,12},{12,8},{16,20},{20,16},{24,28},{28,24},{1,5},{5... | collective-permute-start | bytes 3145736 | tf_op jit(solution)/shard_map/ppermute | solution.py:115
  735.8 34.2 %collective-permute-start.17 = (bf16[256,512]{1,0:T(8,128)(2,1)S(1)}, bf16[256,512]{1,0:T(8,128)(2,1)S(1)}, u32[]{:S(2)}, u32[]{:S(2)}) collective-permute-start(bf16[256,512]{1,0:T(8,128)(2,1)S(1)} %get-tuple-element.57), channel_id=1, source_target_pairs={{0,8},{4,12},{8,0},{12,4},{16,24},{20,28},{24,16},{28,20},{1,9},{5... | collective-permute-start | bytes 786440 | tf_op jit(solution)/shard_map/ppermute | solution.py:115
  736.2 33.9 %collective-permute-start.18 = (bf16[256,512]{1,0:T(8,128)(2,1)S(1)}, bf16[256,512]{1,0:T(8,128)(2,1)S(1)}, u32[]{:S(2)}, u32[]{:S(2)}) collective-permute-start(bf16[256,512]{1,0:T(8,128)(2,1)S(1)} %get-tuple-element.56), channel_id=1, source_target_pairs={{0,16},{4,20},{8,24},{12,28},{16,0},{20,4},{24,8},{28,12},{1,17},{... | collective-permute-start | bytes 786440 | tf_op jit(solution)/shard_map/ppermute | solution.py:115
  739.0 32.3 %collective-permute-start.19 = (bf16[256,512]{1,0:T(8,128)(2,1)S(1)}, bf16[256,512]{1,0:T(8,128)(2,1)S(1)}, u32[]{:S(2)}, u32[]{:S(2)}) collective-permute-start(bf16[256,512]{1,0:T(8,128)(2,1)S(1)} %get-tuple-element.55), channel_id=1, source_target_pairs={{0,24},{4,28},{8,16},{12,20},{16,8},{20,12},{24,0},{28,4},{1,25},{... | collective-permute-start | bytes 786440 | tf_op jit(solution)/shard_map/ppermute | solution.py:115
  770.0 29.3 %collective-permute-start.23 = (bf16[256,512]{1,0:T(8,128)(2,1)S(1)}, bf16[256,512]{1,0:T(8,128)(2,1)S(1)}, u32[]{:S(2)}, u32[]{:S(2)}) collective-permute-start(bf16[256,512]{1,0:T(8,128)(2,1)S(1)} %get-tuple-element.47), channel_id=1, source_target_pairs={{0,24},{4,28},{8,16},{12,20},{16,8},{20,12},{24,0},{28,4},{1,25},{... | collective-permute-start | bytes 786440 | tf_op jit(solution)/shard_map/ppermute | solution.py:115
  770.1 29.2 %collective-permute-start.25 = (bf16[512,256]{1,0:T(8,128)(2,1)S(1)}, bf16[512,256]{1,0:T(8,128)(2,1)S(1)}, u32[]{:S(2)}, u32[]{:S(2)}) collective-permute-start(bf16[512,256]{1,0:T(8,128)(2,1)S(1)} %get-tuple-element.41), channel_id=1, source_target_pairs={{0,8},{4,12},{8,0},{12,4},{16,24},{20,28},{24,16},{28,20},{1,9},{5... | collective-permute-start | bytes 786440 | tf_op jit(solution)/shard_map/ppermute | solution.py:115
  771.4 33.5 %collective-permute-start.26 = (bf16[512,256]{1,0:T(8,128)(2,1)S(1)}, bf16[512,256]{1,0:T(8,128)(2,1)S(1)}, u32[]{:S(2)}, u32[]{:S(2)}) collective-permute-start(bf16[512,256]{1,0:T(8,128)(2,1)S(1)} %get-tuple-element.40), channel_id=1, source_target_pairs={{0,16},{4,20},{8,24},{12,28},{16,0},{20,4},{24,8},{28,12},{1,17},{... | collective-permute-start | bytes 786440 | tf_op jit(solution)/shard_map/ppermute | solution.py:115
  772.9 37.6 %collective-permute-start.27 = (bf16[512,256]{1,0:T(8,128)(2,1)S(1)}, bf16[512,256]{1,0:T(8,128)(2,1)S(1)}, u32[]{:S(2)}, u32[]{:S(2)}) collective-permute-start(bf16[512,256]{1,0:T(8,128)(2,1)S(1)} %get-tuple-element.39), channel_id=1, source_target_pairs={{0,24},{4,28},{8,16},{12,20},{16,8},{20,12},{24,0},{28,4},{1,25},{... | collective-permute-start | bytes 786440 | tf_op jit(solution)/shard_map/ppermute | solution.py:115
  (68 other events, 827.5 us)
Sparse Core Ops, SparseCore 0:
  9.6 24.1 all-gather.11
  70.3 32.6 reduce-scatter.4
  106.6 22.9 all-gather.13
  158.3 31.0 reduce-scatter.6
  194.4 22.9 all-gather.15
  250.6 31.0 reduce-scatter.8
  283.9 44.0 all-gather.19
  330.3 23.5 all-gather.17
  356.1 43.6 all-gather.23
  401.3 59.2 all-gather.21
  464.5 53.8 all-gather.27
  521.4 30.9 reduce-scatter.10
  554.0 58.6 all-gather.25
